TPU v7x, 512 devices: a whole 4x4x16 slice. The times are simulated.
512 devices in a mesh: net: 16 (over z), seg: 8 (over y, core), corner: 4 (over x).
Axes of the slice: x: 4, y: 4, z: 16, core: 2. Of those that a mesh axis runs over, the one named last changes fastest.
Arguments:
- tile_values: bfloat16 [8192, 128, 1024], P(('net', 'seg', 'corner')), may hold values from -48 to 48
- tile_coords: int32 [8192, 3], P(('net', 'seg', 'corner')), may hold values from 0 to 511, as said below
- tile_count: int32 [512], P(('net', 'seg', 'corner')), may hold values from 12 to 16, as said below
- owner_map: int32 [512], P('net'), may hold values from 0 to 511, as said below
- corner_factor: bfloat16 [64, 256], P('corner')
- seg_factor: bfloat16 [65536, 256], P(('seg', 'net'))
Outputs:
- net_factor: float32 [65536, 256], P(('net', 'seg', 'corner'))
Inputs may be any that keep to these rules, and one draw needn't show every extreme that they name: `tile_coords`: row t of device d gives a corner block within the corner range stored by d's corner index, a net block that owner_map assigns to an owner slot of d's net index, and a segment block within the segment range of d's seg index. Among a device's 16 rows at most 2 name segment blocks stored by any one device of the net axis, and on every device two live rows name segment blocks stored by the same device of the net axis. The first tile_count[d] rows of device d are live; the others are ignored. `owner_map`: A permutation of the 512 net blocks.
All inputs are finite; a program needn't handle non-finite values.
Results may differ from a plain program's by a relative error of at most 0.0058.
The roundings to bfloat16 on the way count: a program that leaves them out, or rounds other values in their place, can miss the bound.
Values may be sent and summed in bfloat16 or wider, within the bound.
No kernel may reach another device: no remote copies, remote signals or barrier semaphores. Data moves between devices by JAX's collectives and lax.ppermute only.
A program may use at most 64 MiB of HBM per device.

v0:
```python
import jax
import jax.numpy as jnp
from jax import lax
from jax.sharding import PartitionSpec as P

CBLK = 8
GRP = 4


def solve_rows(gram, mttkrp):
    cholesky_low = jnp.linalg.cholesky(gram)
    forward = lax.linalg.triangular_solve(cholesky_low, mttkrp.T, left_side=True, lower=True)
    backward = lax.linalg.triangular_solve(
        cholesky_low, forward, left_side=True, lower=True, transpose_a=True
    )
    return backward.T


def contract(packed):
    values, corner_rows, seg_rows = packed
    khatri = (
        corner_rows.astype(jnp.float32)[:, :, None, :] * seg_rows.astype(jnp.float32)[:, None, :, :]
    ).astype(jnp.bfloat16)
    khatri = khatri.reshape(values.shape[0], values.shape[2], corner_rows.shape[2])
    return jnp.einsum("tnj,tjr->tnr", values, khatri, preferred_element_type=jnp.float32)


def body(tile_values, tile_coords, tile_count, owner_map, corner_factor, seg_factor):
    slot_total = tile_values.shape[0]
    net_rows = tile_values.shape[1]
    columns = corner_factor.shape[1]
    seg_width = tile_values.shape[2] // CBLK
    held_blocks = seg_factor.shape[0] // seg_width
    net_devices = lax.axis_size("net")
    corner_local = tile_coords[:, 0] - lax.axis_index("corner") * (corner_factor.shape[0] // CBLK)
    seg_local = tile_coords[:, 2] - lax.axis_index("seg") * (held_blocks * net_devices)
    corner_sel = jnp.take(corner_factor.reshape(-1, CBLK, columns), corner_local, axis=0)
    gathered = lax.all_gather(seg_factor, "net", axis=0, tiled=True)
    seg_sel = jnp.take(gathered.reshape(-1, seg_width, columns), seg_local, axis=0)
    groups = slot_total // GRP
    partial_value = lax.map(
        contract,
        (
            tile_values.reshape(groups, GRP, net_rows, -1),
            corner_sel.reshape(groups, GRP, CBLK, columns),
            seg_sel.reshape(groups, GRP, seg_width, columns),
        ),
    )
    partial_value = partial_value.reshape(slot_total, net_rows * columns)
    live_mask = jnp.arange(slot_total, dtype=jnp.int32) < tile_count[0]
    member = ((tile_coords[:, 1][:, None] == owner_map[None, :]) & live_mask[:, None]).astype(
        jnp.float32
    )
    summed = jnp.dot(
        member.T, partial_value, precision=lax.Precision.HIGHEST, preferred_element_type=jnp.float32
    )
    mttkrp = lax.psum_scatter(
        summed.reshape(net_rows * lax.axis_size(("seg", "corner")), columns),
        ("seg", "corner"),
        scatter_dimension=0,
        tiled=True,
    )
    corner_part = jnp.dot(corner_factor.T, corner_factor, preferred_element_type=jnp.float32)
    seg_part = jnp.dot(seg_factor.T, seg_factor, preferred_element_type=jnp.float32)
    seg_gram = lax.psum(seg_part, ("net", "seg"))
    corner_gram = lax.psum(corner_part, "corner")
    return solve_rows(corner_gram * seg_gram, mttkrp)


def solution(mesh):
    return jax.shard_map(
        body,
        mesh=mesh,
        in_specs=(
            P(("net", "seg", "corner"), None, None),
            P(("net", "seg", "corner"), None),
            P(("net", "seg", "corner")),
            P("net"),
            P("corner", None),
            P(("seg", "net"), None),
        ),
        out_specs=P(("net", "seg", "corner"), None),
        check_vma=False,
    )
```

profile of v0, /device:TPU:8, one launch (start us, length us, event | category | flops | bytes accessed | tf_op | source)
XLA Modules:
  0.0 481.0 jit_solution(18225845388589294858)
XLA Ops:
  7.4 0.0 copy-start
  7.4 0.0 all-gather.2.cloned.1.call-start
  7.4 0.7 all-gather.2.cloned.1.call-update
  8.1 0.0 all-reduce.6.cloned.1.call-start
  8.1 2.1 fusion.23
  10.2 0.0 all-reduce.6.cloned.1.call-update
  10.3 0.0 all-reduce.4.cloned.1.call-start
  10.3 0.0 copy-done
  10.3 1.0 fusion.22
  11.3 0.0 all-reduce.4.cloned.1.call-update
  11.3 0.0 reduce-scatter.2.cloned.1.call-start
  11.4 0.7 slice_bitcast_fusion.6
  12.1 0.8 and_reduce_fusion
  12.8 0.1 broadcast_in_dim.38
  12.9 0.1 broadcast_in_dim.41
  13.7 0.6 gather_fusion
  14.3 0.1 broadcast_select_fusion.1
  14.3 79.2 %all-gather.2.cloned.1.call-done = bf16[8192,256]{1,0:T(8,128)(2,1)} async-done(((bf16[512,256]{1,0:T(8,128)(2,1)}), bf16[8192,256]{1,0:T(8,128)(2,1)}) %all-gather.2.cloned.1.call-update) | async-done | bytes 4194320 | tf_op jit(solution)/shard_map/all_gather | solution.py:38
  93.5 2.8 gather_fusion.1
  96.4 0.2 broadcast_select_fusion
  96.5 12.6 %while.11 = (s32[]{:T(128)}, f32[4,4,128,256]{3,2,1,0:T(8,128)}, bf16[4,4,128,1024]{3,2,1,0:T(8,128)(2,1)}, bf16[4,4,8,256]{3,2,1,0:T(8,128)(2,1)S(1)}, bf16[4,4,128,256]{3,2,1,0:T(8,128)(2,1)S(1)}, /*index=5*/s32[]{:T(128)}) while((s32[]{:T(128)}, f32[4,4,128,256]{3,2,1,0:T(8,128)}, bf16[4,4,128,1024]{3,2,1,0:T(8,128)(2,1)}, ...), condition=%wide.region_7.8_spmd, body=%wide.region_6.7_spmd.sunk | while | flops 270671872 | bytes 7160917 | solution.py:41
  96.6 0.6 multiply_convert_fusion.2
  97.2 2.5 fusion.43
  99.7 0.6 multiply_convert_fusion.2
  100.3 2.5 fusion.43
  102.9 0.6 multiply_convert_fusion.2
  103.5 2.5 fusion.43
  106.0 0.6 multiply_convert_fusion.2
  106.6 2.5 fusion.43
  109.1 0.0 copy-start.1
  109.1 2.8 copy.13
  111.9 0.0 copy-done.1
  111.9 3.5 fusion.15
  115.5 4.9 %reshape.80 = f32[4096,256]{1,0:T(8,128)} reshape(f32[32,32768]{1,0:T(8,128)} %fusion.15) | data formatting | bytes 8388608 | tf_op jit(solution)/shard_map/reshape | solution.py:58
  120.4 0.0 reduce-scatter.2.cloned.1.call-update
  120.4 232.0 %all-reduce.6.cloned.1.call-done = f32[256,256]{0,1:T(8,128)} async-done(((f32[256,256]{0,1:T(8,128)}), f32[256,256]{0,1:T(8,128)}) %all-reduce.6.cloned.1.call-update) | async-done | bytes 262160 | tf_op jit(solution)/shard_map/psum | solution.py:65
  352.4 56.2 %all-reduce.4.cloned.1.call-done = f32[256,256]{0,1:T(8,128)} async-done(((f32[256,256]{0,1:T(8,128)}), f32[256,256]{0,1:T(8,128)}) %all-reduce.4.cloned.1.call-update) | async-done | bytes 262160 | tf_op jit(solution)/shard_map/psum | solution.py:66
  408.6 1.1 mul.24
  409.6 0.1 copy.9
  409.8 11.7 %cholesky.50 = f32[128,128]{1,0:T(8,128)S(1)} custom-call(f32[128,128]{1,0:T(8,128)S(1)} %cholesky.118), custom_call_target="Cholesky" | custom-call | tf_op jit(solution)/shard_map/jit(cholesky)/cholesky | solution.py:11
  421.6 9.8 %custom-call.16 = f32[1,128,128]{1,2,0:T(8,128)S(1)} custom-call(f32[1,128,128]{2,1,0:T(8,128)S(1)} %get-tuple-element.68), custom_call_target="InvertDiagBlocksLowerTriangular" | custom-call | tf_op jit(solution)/shard_map/jit(cholesky)/cholesky | solution.py:11
  431.4 0.2 constant_dynamic-update-slice_fusion.1
  431.6 0.3 convolution_subtract_fusion.2
  431.9 11.7 %cholesky.105 = f32[128,128]{1,0:T(8,128)S(1)} custom-call(f32[128,128]{1,0:T(8,128)S(1)} %convolution_subtract_fusion.2), custom_call_target="Cholesky" | custom-call | tf_op jit(solution)/shard_map/jit(cholesky)/cholesky | solution.py:11
  443.7 0.7 compare_reduce_fusion
  445.6 0.1 triangular_solve.66
  445.7 3.9 while.12
  445.7 0.6 fusion.44
  446.3 1.3 bitcast_dynamic-update-slice_fusion.2
  447.7 0.6 fusion.44
  448.3 1.3 bitcast_dynamic-update-slice_fusion.2
  449.6 19.9 %custom-call.17 = f32[2,128,128]{1,2,0:T(8,128)S(1)} custom-call(f32[2,128,128]{2,1,0:T(8,128)S(1)} %get-tuple-element.40), custom_call_target="InvertDiagBlocksLowerTriangular" | custom-call | tf_op jit(solution)/shard_map/triangular_solve | solution.py:13
  469.5 0.0 reduce-scatter.2.cloned.1.call-done
  469.5 1.1 fusion.5
  470.7 1.1 convolution_subtract_fusion.1
  471.8 0.3 fusion.12
  472.1 0.2 fusion.11
  472.3 0.3 convolution_subtract_fusion
  472.6 0.2 fusion.10
  472.8 0.8 copy.10
  (23 shorter events, 0.4 us)
Async XLA Ops:
  7.4 2.9 copy-start
  7.4 86.2 %all-gather.2.cloned.1.call-start = ((), (), s32[]{:S(2)}) async-start(), calls=%async_computation.3 | async-start | bytes 4456448 | tf_op jit(solution)/shard_map/all_gather | solution.py:38
  8.1 344.3 %all-reduce.6.cloned.1.call-start = ((), (), s32[]{:S(2)}) async-start(), calls=%async_computation.2 | async-start | bytes 524288 | tf_op jit(solution)/shard_map/psum | solution.py:65
  10.3 398.3 %all-reduce.4.cloned.1.call-start = ((), (), s32[]{:S(2)}) async-start(), calls=%async_computation.1 | async-start | bytes 524288 | tf_op jit(solution)/shard_map/psum | solution.py:66
  11.3 458.2 %reduce-scatter.2.cloned.1.call-start = ((), (), s32[]{:S(2)}) async-start(), calls=%async_computation.4 | async-start | bytes 4325376 | tf_op jit(solution)/shard_map/reduce_scatter | solution.py:57
  109.1 2.8 copy-start.1
Sparse Core Ops, SparseCore 0:
  10.3 83.2 all-gather.1
  120.5 101.2 reduce-scatter.1
Sparse Core Ops, SparseCore 1:
  12.4 339.9 all-reduce.5
  354.7 53.8 all-reduce.3
where the time goes:
time: 482 us; the launch traced here: 481 us
  waiting for transfers between devices  368 us (76%)
  other arithmetic  58.6 us (12%)
  matrix products  20.2 us (4%)
  between operations  17 us (4%)
  local copies, waits for them, and re-layouts  16.8 us (3%)
    psum x1, waiting for transfers between devices, body(): seg_gram = lax.psum(seg_part, ('net', 'seg'))  232 us
    all_gather x1, waiting for transfers between devices, body(): gathered = lax.all_gather(seg_factor, 'net', axis=0, tiled=True)  79.2 us
    psum x1, waiting for transfers between devices, body(): corner_gram = lax.psum(corner_part, 'corner')  56.2 us
    another operation x6, other arithmetic, solve_rows(): cholesky_low = jnp.linalg.cholesky(gram)  34 us
    another operation x3, other arithmetic, solve_rows(): lax.linalg.triangular_solve(cholesky_low, forward, left_side=True, lower=...  19.9 us
    dot_general x4, matrix products, contract(): jnp.einsum('tnj,tjr->tnr', values, khatri, preferred_element_type=jnp.flo...  9.96 us
  transfers between devices with their start and end apart: 4, of which 3 were waited for; matrix products, arithmetic and copies ran while one was open for 19% of the time, Pallas kernels for 0%

commit v1 on v0

--- a/solution.py
+++ b/solution.py
@@ -5,6 +5,12 @@
 
 CBLK = 8
 GRP = 4
+
+
+def set_row_by_axis(axis_id, shard_in):
+    w1 = jax.lax.all_gather(shard_in, axis_name=axis_id)
+    finding = jnp.sum(w1, axis=0)
+    return finding
 
 
 def solve_rows(gram, mttkrp):
@@ -63,7 +69,7 @@
     corner_part = jnp.dot(corner_factor.T, corner_factor, preferred_element_type=jnp.float32)
     seg_part = jnp.dot(seg_factor.T, seg_factor, preferred_element_type=jnp.float32)
     seg_gram = lax.psum(seg_part, ("net", "seg"))
-    corner_gram = lax.psum(corner_part, "corner")
+    corner_gram = set_row_by_axis("corner", corner_part)
     return solve_rows(corner_gram * seg_gram, mttkrp)
 
 

time: 482 us -> 426 us (0.88)
  the two profiles are of different devices: /device:TPU:8 before, /device:TPU:1 now
where the time goes in v1:
time: 426 us; the launch traced here: 425 us
  waiting for transfers between devices  311 us (73%)
  other arithmetic  59.8 us (14%)
  matrix products  20.2 us (5%)
  local copies, waits for them, and re-layouts  17 us (4%)
  between operations  16.7 us (4%)
    psum x1, waiting for transfers between devices, body(): seg_gram = lax.psum(seg_part, ('net', 'seg'))  228 us
    all_gather x1, waiting for transfers between devices, body(): gathered = lax.all_gather(seg_factor, 'net', axis=0, tiled=True)  72 us
    another operation x6, other arithmetic, solve_rows(): cholesky_low = jnp.linalg.cholesky(gram)  34 us
    another operation x3, other arithmetic, solve_rows(): lax.linalg.triangular_solve(cholesky_low, forward, left_side=True, lower=...  19.9 us
    all_gather x1, waiting for transfers between devices, set_row_by_axis(): w1 = jax.lax.all_gather(shard_in, axis_name=axis_id)  10.6 us
    dot_general x4, matrix products, contract(): jnp.einsum('tnj,tjr->tnr', values, khatri, preferred_element_type=jnp.flo...  9.96 us
  transfers between devices with their start and end apart: 4, of which 3 were waited for; matrix products, arithmetic and copies ran while one was open for 22% of the time, Pallas kernels for 0%

profile of v1, /device:TPU:1, one launch (start us, length us, event | category | flops | bytes accessed | tf_op | source)
XLA Modules:
  0.0 425.2 jit_solution(6976329644886090397)
XLA Ops:
  7.4 0.0 copy-start
  7.4 0.0 all-gather.4.cloned.1.call-start
  7.4 0.7 all-gather.4.cloned.1.call-update
  8.1 0.0 all-gather.6.cloned.1.call-start
  8.1 0.0 copy-done
  8.1 0.9 fusion.22
  9.1 0.0 all-gather.6.cloned.1.call-update
  9.1 0.0 all-reduce.3.cloned.1.call-start
  9.2 2.0 fusion.23
  11.2 0.0 all-reduce.3.cloned.1.call-update
  11.2 0.0 reduce-scatter.2.cloned.1.call-start
  11.3 0.7 slice_bitcast_fusion.6
  12.0 0.8 and_reduce_fusion
  12.8 0.1 broadcast_in_dim.38
  12.9 0.1 broadcast_in_dim.41
  13.6 0.6 gather_fusion
  14.2 0.1 broadcast_select_fusion.1
  14.3 72.0 %all-gather.4.cloned.1.call-done = bf16[8192,256]{1,0:T(8,128)(2,1)} async-done(((bf16[512,256]{1,0:T(8,128)(2,1)}), bf16[8192,256]{1,0:T(8,128)(2,1)}) %all-gather.4.cloned.1.call-update) | async-done | bytes 4194320 | tf_op jit(solution)/shard_map/all_gather | solution.py:44
  86.3 2.8 gather_fusion.1
  89.1 0.2 broadcast_select_fusion
  89.3 12.6 %while.11 = (s32[]{:T(128)}, f32[4,4,128,256]{3,2,1,0:T(8,128)}, bf16[4,4,128,1024]{3,2,1,0:T(8,128)(2,1)}, bf16[4,4,8,256]{3,2,1,0:T(8,128)(2,1)S(1)}, bf16[4,4,128,256]{3,2,1,0:T(8,128)(2,1)S(1)}, /*index=5*/s32[]{:T(128)}) while((s32[]{:T(128)}, f32[4,4,128,256]{3,2,1,0:T(8,128)}, bf16[4,4,128,1024]{3,2,1,0:T(8,128)(2,1)}, ...), condition=%wide.region_7.8_spmd, body=%wide.region_6.7_spmd.sunk | while | flops 270671872 | bytes 7160917 | solution.py:47
  89.4 0.6 multiply_convert_fusion.2
  90.0 2.5 fusion.43
  92.5 0.6 multiply_convert_fusion.2
  93.1 2.5 fusion.43
  95.7 0.6 multiply_convert_fusion.2
  96.2 2.5 fusion.43
  98.8 0.6 multiply_convert_fusion.2
  99.4 2.5 fusion.43
  101.9 0.0 copy-start.1
  101.9 2.8 copy.15
  104.7 0.0 copy-done.1
  104.7 3.5 fusion.15
  108.2 5.0 %reshape.80 = f32[4096,256]{1,0:T(8,128)} reshape(f32[32,32768]{1,0:T(8,128)} %fusion.15) | data formatting | bytes 8388608 | tf_op jit(solution)/shard_map/reshape | solution.py:64
  113.2 0.0 reduce-scatter.2.cloned.1.call-update
  113.3 10.6 %all-gather.6.cloned.1.call-done = f32[1024,256]{1,0:T(8,128)} async-done(((f32[256,256]{1,0:T(8,128)}), f32[1024,256]{1,0:T(8,128)}) %all-gather.6.cloned.1.call-update) | async-done | bytes 1048592 | tf_op jit(solution)/shard_map/all_gather | solution.py:11
  123.8 1.3 reduce_sum.9
  125.2 0.1 copy.11
  125.3 227.8 %all-reduce.3.cloned.1.call-done = f32[256,256]{0,1:T(8,128)} async-done(((f32[256,256]{0,1:T(8,128)}), f32[256,256]{0,1:T(8,128)}) %all-reduce.3.cloned.1.call-update) | async-done | bytes 262160 | tf_op jit(solution)/shard_map/psum | solution.py:71
  353.1 1.0 mul.24
  354.1 0.1 copy.12
  354.3 11.7 %cholesky.50 = f32[128,128]{1,0:T(8,128)S(1)} custom-call(f32[128,128]{1,0:T(8,128)S(1)} %cholesky.118), custom_call_target="Cholesky" | custom-call | tf_op jit(solution)/shard_map/jit(cholesky)/cholesky | solution.py:17
  366.1 9.8 %custom-call.16 = f32[1,128,128]{1,2,0:T(8,128)S(1)} custom-call(f32[1,128,128]{2,1,0:T(8,128)S(1)} %get-tuple-element.68), custom_call_target="InvertDiagBlocksLowerTriangular" | custom-call | tf_op jit(solution)/shard_map/jit(cholesky)/cholesky | solution.py:17
  375.9 0.2 constant_dynamic-update-slice_fusion.1
  376.1 0.3 convolution_subtract_fusion.2
  376.4 11.7 %cholesky.105 = f32[128,128]{1,0:T(8,128)S(1)} custom-call(f32[128,128]{1,0:T(8,128)S(1)} %convolution_subtract_fusion.2), custom_call_target="Cholesky" | custom-call | tf_op jit(solution)/shard_map/jit(cholesky)/cholesky | solution.py:17
  388.1 0.7 compare_reduce_fusion
  390.0 0.1 triangular_solve.66
  390.1 3.9 while.12
  390.1 0.6 fusion.44
  390.7 1.3 bitcast_dynamic-update-slice_fusion.2
  392.1 0.6 fusion.44
  392.7 1.3 bitcast_dynamic-update-slice_fusion.2
  394.0 19.9 %custom-call.17 = f32[2,128,128]{1,2,0:T(8,128)S(1)} custom-call(f32[2,128,128]{2,1,0:T(8,128)S(1)} %get-tuple-element.40), custom_call_target="InvertDiagBlocksLowerTriangular" | custom-call | tf_op jit(solution)/shard_map/triangular_solve | solution.py:19
  413.9 0.0 reduce-scatter.2.cloned.1.call-done
  414.0 1.1 fusion.5
  415.1 1.1 convolution_subtract_fusion.1
  416.2 0.3 fusion.12
  416.5 0.2 fusion.11
  416.7 0.3 convolution_subtract_fusion
  417.0 0.2 fusion.10
  417.3 0.8 copy.13
  (23 shorter events, 0.4 us)
Async XLA Ops:
  7.4 0.8 copy-start
  7.4 78.9 %all-gather.4.cloned.1.call-start = ((), (), s32[]{:S(2)}) async-start(), calls=%async_computation.2 | async-start | bytes 4456448 | tf_op jit(solution)/shard_map/all_gather | solution.py:44
  8.1 115.8 %all-gather.6.cloned.1.call-start = ((), (), s32[]{:S(2)}) async-start(), calls=%async_computation.4 | async-start | bytes 1310720 | tf_op jit(solution)/shard_map/all_gather | solution.py:11
  9.1 344.0 %all-reduce.3.cloned.1.call-start = ((), (), s32[]{:S(2)}) async-start(), calls=%async_computation.1 | async-start | bytes 524288 | tf_op jit(solution)/shard_map/psum | solution.py:71
  11.2 402.7 %reduce-scatter.2.cloned.1.call-start = ((), (), s32[]{:S(2)}) async-start(), calls=%async_computation.3 | async-start | bytes 4325376 | tf_op jit(solution)/shard_map/reduce_scatter | solution.py:63
  101.9 2.8 copy-start.1
Sparse Core Ops, SparseCore 0:
  10.3 75.9 all-gather.3
  88.4 35.3 all-gather.5
  128.4 104.7 reduce-scatter.1
Sparse Core Ops, SparseCore 1:
  13.4 339.6 all-reduce.2
